TPU v7x, 32 devices: a whole 2x2x4 slice. The times are simulated.
32 devices in a mesh: seq: 8 (over z, x), head: 4 (over y, core).
Axes of the slice: x: 2, y: 2, z: 4, core: 2. Of those that a mesh axis runs over, the one named last changes fastest.
Arguments:
- queries: float32 [8192, 4096], P('seq', 'head'), may hold values from -6 to 6
- keys: float32 [8192, 4096], P('seq', 'head'), may hold values from -6 to 6
- values: float32 [8192, 4096], P('seq', 'head'), may hold values from -6 to 6
- out_grad: float32 [8192, 4096], P('seq', 'head'), may hold values from -6 to 6
- inputs: float32 [8192, 4096], P('seq', 'head'), may hold values from -20 to 20
- row_state: float32 [4, 4096], P('head', 'seq'), may hold values from 0.2 to 5
- col_state: float32 [8, 4096], P('seq', 'head'), may hold values from 0.2 to 5
Outputs:
- query_grad: float32 [8192, 4096], P('seq', 'head')
- key_grad: float32 [8192, 4096], P('seq', 'head')
- update: float32 [4096, 4096], P('seq', 'head')
- row_next: float32 [4, 4096], P('head', 'seq')
- col_next: float32 [8, 4096], P('seq', 'head')
All inputs are finite; a program needn't handle non-finite values.
Results may differ from a plain program's by a relative error of at most 0.0001.
Values sent between devices are 32-bit elements; how exact they have to be, the bound alone decides.
No kernel may reach another device: no remote copies, remote signals or barrier semaphores. Data moves between devices by JAX's collectives and lax.ppermute only.
A program may use at most 128 MiB of HBM per device.

v0:
```python
import jax
import jax.numpy as jnp
from jax import lax
from jax.sharding import PartitionSpec as P

HEAD_DIM = 128
highest = lax.Precision.HIGHEST
moment_eps = 1e-06
decay_rate = 0.9


def shards(queries, keys, values, out_grad, inputs, row_state, col_state):
    tok_count, feat_width = queries.shape
    head_count = feat_width // HEAD_DIM
    seq_count = lax.axis_size("seq")
    blk_size = min(512, tok_count)
    num_blocks = tok_count // blk_size
    attn_scale = 1.0 / jnp.sqrt(jnp.float32(HEAD_DIM * tok_count * seq_count))

    def split_blocks(array):
        return array.reshape(num_blocks, blk_size, head_count, HEAD_DIM)

    query_blocks = split_blocks(queries)
    key_blocks = split_blocks(keys)
    value_blocks = split_blocks(values)
    grad_blocks = split_blocks(out_grad)
    rows_idx = lax.broadcasted_iota(jnp.int32, (blk_size, blk_size), 0)
    cols_idx = lax.broadcasted_iota(jnp.int32, (blk_size, blk_size), 1)
    causal_mask = (cols_idx <= rows_idx).astype(jnp.float32)
    grad_value = (
        jnp.einsum("nthd,nshd->nhts", grad_blocks, value_blocks, precision=highest) * causal_mask
    )
    query_key = (
        jnp.einsum("nthd,nshd->nhts", query_blocks, key_blocks, precision=highest) * causal_mask
    )
    block_fwd = jnp.einsum("nsha,nshb->nhab", value_blocks, key_blocks, precision=highest)
    block_rev = jnp.einsum("ntha,nthb->nhab", query_blocks, grad_blocks, precision=highest)
    local_fwd = jnp.sum(block_fwd, axis=0)
    local_rev = jnp.sum(block_rev, axis=0)
    every_fwd, every_rev = (
        lax.all_gather(local_fwd[None], "seq", axis=0, tiled=True),
        lax.all_gather(local_rev[None], "seq", axis=0, tiled=True),
    )
    seq_index = lax.axis_index("seq")
    positions = lax.iota(jnp.int32, every_fwd.shape[0])
    before = (positions < seq_index).astype(jnp.float32)
    after = (positions > seq_index).astype(jnp.float32)
    enter_fwd = jnp.einsum("j,jhab->hab", before, every_fwd, precision=highest)
    enter_rev = jnp.einsum("j,jhab->hab", after, every_rev, precision=highest)
    prefix_fwd = enter_fwd[None] + jnp.cumsum(block_fwd, axis=0) - block_fwd
    suffix_rev = enter_rev[None] + local_rev[None] - jnp.cumsum(block_rev, axis=0)
    query_grad = jnp.einsum("nhts,nshd->nthd", grad_value, key_blocks, precision=highest)
    query_grad = query_grad + jnp.einsum(
        "ntha,nhab->nthb", grad_blocks, prefix_fwd, precision=highest
    )
    key_grad = jnp.einsum("nhts,nthd->nshd", grad_value, query_blocks, precision=highest)
    key_grad = key_grad + jnp.einsum("nshb,nhab->nsha", value_blocks, suffix_rev, precision=highest)
    value_grad = jnp.einsum("nhts,nthd->nshd", query_key, grad_blocks, precision=highest)
    value_grad = value_grad + jnp.einsum(
        "nsha,nhab->nshb", key_blocks, suffix_rev, precision=highest
    )
    query_grad = (attn_scale * query_grad).reshape(tok_count, feat_width)
    key_grad = (attn_scale * key_grad).reshape(tok_count, feat_width)
    value_grad = (attn_scale * value_grad).reshape(tok_count, feat_width)
    value_whole = lax.all_gather(value_grad, "head", axis=1, tiled=True)
    weight_grad = lax.psum_scatter(
        lax.dot_general(
            value_whole,
            inputs,
            (((0,), (0,)), ((), ())),
            precision=highest,
            preferred_element_type=jnp.float32,
        ),
        "seq",
        scatter_dimension=0,
        tiled=True,
    )
    weight_grad = weight_grad / jnp.sqrt(jnp.float32(tok_count * seq_count))
    squares = weight_grad * weight_grad + moment_eps
    row_next = decay_rate * row_state + (1.0 - decay_rate) * jnp.mean(squares, axis=1)[None, :]
    col_next = decay_rate * col_state + (1.0 - decay_rate) * jnp.mean(squares, axis=0)[None, :]
    second = row_next[0][:, None] * col_next[0][None, :] / jnp.mean(row_next)
    update = weight_grad / jnp.sqrt(second)
    return (query_grad, key_grad, update, row_next, col_next)


def solution(mesh):
    in_specs = (
        P("seq", "head"),
        P("seq", "head"),
        P("seq", "head"),
        P("seq", "head"),
        P("seq", "head"),
        P("head", "seq"),
        P("seq", "head"),
    )
    out_specs = (
        P("seq", "head"),
        P("seq", "head"),
        P("seq", "head"),
        P("head", "seq"),
        P("seq", "head"),
    )
    return jax.shard_map(shards, mesh=mesh, in_specs=in_specs, out_specs=out_specs, check_vma=False)
```

profile of v0, /device:TPU:0, one launch (start us, length us, event | category | flops | bytes accessed | tf_op | source)
XLA Modules:
  0.0 588.8 jit_solution(3645238673202636491)
XLA Ops:
  7.2 0.0 all-gather.10.cloned.1.call-start
  7.2 3.4 copy.90
  10.6 0.0 copy-start
  10.6 0.1 copy-done.15
  10.7 1.0 copy.94
  11.7 0.9 copy-done
  12.7 8.4 %fusion.57 = (f32[8,128,128]{2,1,0:T(8,128)}, f32[2,8,128,128]{3,2,1,0:T(8,128)S(1)}) fusion(f32[2,512,8,128]{3,2,1,0:T(8,128)S(1)} %bitcast.70, f32[2,512,8,128]{3,2,1,0:T(8,128)S(1)} %bitcast.81), kind=kOutput, calls=%fused_computation.66 | convolution fusion | flops 1610743808 | bytes 9961472 | tf_op jit(solution)/shard_map/ntha,nthb->nhab/dot_general | solution.py:37
  21.1 0.0 all-gather.10.cloned.1.call-update
  21.1 0.2 all-gather.6.cloned.1.call-start
  21.4 3.4 copy.92
  24.7 0.1 fusion.46
  24.9 1.8 copy-done.3
  26.7 16.0 %fusion.18 = f32[2,8,512,512]{3,2,1,0:T(8,128)} fusion(f32[2,512,8,128]{3,2,1,0:T(8,128)S(1)} %bitcast.83, f32[2,512,8,128]{3,2,1,0:T(8,128)S(1)} %bitcast.74), kind=kOutput, calls=%fused_computation.24 | convolution fusion | flops 6442450944 | bytes 25165824 | tf_op jit(solution)/shard_map/nthd,nshd->nhts/dot_general | solution.py:34
  42.6 31.1 %fusion = f32[2,8,512,128]{3,2,1,0:T(8,128)} fusion(f32[2,8,512,512]{3,2,1,0:T(8,128)} %fusion.18, f32[512,512]{1,0:T(8,128)S(1)} %fusion.46, f32[2,512,8,128]{3,2,1,0:T(8,128)S(1)} %bitcast.72), kind=kOutput, calls=%fused_computation | convolution fusion | flops 6446645248 | bytes 26214400 | tf_op jit(solution)/shard_map/nhts,nthd->nshd/dot_general | solution.py:58
  73.7 0.0 copy-start.14
  73.7 23.1 %all-gather.10.cloned.1.call-done = f32[64,128,128]{2,1,0:T(8,128)} async-done(((f32[8,128,128]{2,1,0:T(8,128)}), f32[64,128,128]{2,1,0:T(8,128)}) %all-gather.10.cloned.1.call-update) | async-done | bytes 4194320 | tf_op jit(solution)/shard_map/all_gather | solution.py:42
  96.8 6.6 %fusion.12 = f32[1,8,128,128]{3,0,2,1:T(1,128)S(1)} fusion(f32[8,8,128,128]{3,2,1,0:T(8,128)} %bitcast.89, s32[]{:T(128)S(6)} %axis_index.15), kind=kOutput, calls=%fused_computation.18 | convolution fusion | flops 12582920 | bytes 4718596 | tf_op jit(solution)/shard_map/j,jhab->hab/dot_general | solution.py:49
  103.4 0.1 add.38
  103.5 0.2 reduce-window_subtract_fusion
  103.8 4.4 fusion.9
  108.2 2.4 copy.76
  110.6 2.9 copy.146
  113.6 0.0 all-gather.6.cloned.1.call-update
  113.6 0.4 all-gather.8.cloned.1.call-start
  114.1 3.4 copy.91
  117.4 0.0 copy-start.6
  117.4 0.1 copy-done.5
  117.5 9.5 %fusion.56 = (f32[8,128,128]{2,1,0:T(8,128)}, f32[2,8,128,128]{3,2,1,0:T(8,128)}) fusion(f32[2,512,8,128]{3,2,1,0:T(8,128)S(1)} %bitcast.77, f32[2,512,8,128]{3,2,1,0:T(8,128)S(1)} %bitcast.78), kind=kOutput, calls=%fused_computation.65 | convolution fusion | flops 1610743808 | bytes 9961472 | tf_op jit(solution)/shard_map/nsha,nshb->nhab/dot_general | solution.py:36
  127.0 0.0 all-gather.8.cloned.1.call-update
  127.0 0.0 reduce-scatter.2.cloned.1.call-start
  127.1 91.1 %all-gather.6.cloned.1.call-done = f32[1024,4096]{1,0:T(8,128)} async-done(((f32[1024,1024]{1,0:T(8,128)}), f32[1024,4096]{1,0:T(8,128)}) %all-gather.6.cloned.1.call-update) | async-done | bytes 16777232 | tf_op jit(solution)/shard_map/all_gather | solution.py:65
  218.2 59.7 %fusion.58 = f32[4096,1024]{1,0:T(8,128)} fusion(f32[1024,4096]{1,0:T(8,128)} %all-gather.6.cloned.1.call-done, f32[1024,1024]{1,0:T(8,128)} %param.11), kind=kOutput, calls=%fused_computation.67 | convolution fusion | flops 51539607552 | bytes 37748736 | tf_op jit(solution)/shard_map/dot_general | solution.py:67
  277.9 0.0 reduce-scatter.2.cloned.1.call-update
  277.9 18.8 %fusion.25 = f32[2,8,512,512]{3,2,1,0:T(8,128)S(1)} fusion(f32[2,512,8,128]{3,2,1,0:T(8,128)} %bitcast.79, f32[2,512,8,128]{3,2,1,0:T(8,128)} %bitcast.71), kind=kOutput, calls=%fused_computation.31 | convolution fusion | flops 6442450944 | bytes 25165824 | tf_op jit(solution)/shard_map/nthd,nshd->nhts/dot_general | solution.py:31
  296.8 30.1 %fusion.2 = f32[2,8,512,128]{3,2,1,0:T(8,128)} fusion(f32[2,8,512,512]{3,2,1,0:T(8,128)S(1)} %fusion.25, f32[512,512]{1,0:T(8,128)S(1)} %fusion.46, f32[2,512,8,128]{3,2,1,0:T(8,128)} %bitcast.82), kind=kOutput, calls=%fused_computation.2 | convolution fusion | flops 6446645248 | bytes 26214400 | tf_op jit(solution)/shard_map/nhts,nthd->nshd/dot_general | solution.py:56
  326.8 18.3 %fusion.4 = f32[2,8,512,128]{3,2,1,0:T(8,128)} fusion(f32[2,8,512,512]{3,2,1,0:T(8,128)S(1)} %fusion.25, f32[512,512]{1,0:T(8,128)S(1)} %fusion.46, f32[2,512,8,128]{3,2,1,0:T(8,128)} %bitcast.75), kind=kOutput, calls=%fused_computation.4 | convolution fusion | flops 6446645248 | bytes 26214400 | tf_op jit(solution)/shard_map/nhts,nshd->nthd/dot_general | solution.py:52
  345.1 7.7 %fusion.10 = f32[2,512,8,128]{3,1,2,0:T(8,128)S(1)} fusion(f32[2,8,512,128]{3,2,1,0:T(8,128)} %fusion.2, f32[2,8,128,128]{3,2,1,0:T(8,128)} %copy-done.13, f32[2,512,8,128]{3,2,1,0:T(8,128)} %bitcast.80), kind=kOutput, calls=%fused_computation.15 | convolution fusion | flops 1612709888 | bytes 13631488 | tf_op jit(solution)/shard_map/nshb,nhab->nsha/dot_general | solution.py:57
  352.8 4.4 copy.68
  357.3 6.6 %fusion.14 = f32[1,8,128,128]{3,0,2,1:T(1,128)S(1)} fusion(f32[8,8,128,128]{3,2,1,0:T(8,128)} %bitcast.88, s32[]{:T(128)S(6)} %axis_index.15), kind=kOutput, calls=%fused_computation.20 | convolution fusion | flops 12582920 | bytes 4718596 | tf_op jit(solution)/shard_map/j,jhab->hab/dot_general | solution.py:48
  363.9 0.5 fusion.45
  364.5 4.4 fusion.11
  368.9 0.0 copy-start.10
  368.9 2.4 copy.61
  371.4 5.5 copy_bitcast_fusion.1
  376.9 198.2 %reduce-scatter.2.cloned.1.call-done = f32[512,1024]{1,0:T(8,128)} async-done(((f32[4096,1024]{1,0:T(8,128)}), f32[512,1024]{1,0:T(8,128)}) %reduce-scatter.2.cloned.1.call-update) | async-done | bytes 2097168 | tf_op jit(solution)/shard_map/reduce_scatter | solution.py:66
  575.1 2.1 fusion.43
  577.2 0.6 fusion.55
  578.5 3.3 rsqrt_multiply_fusion
  (36 shorter events, 0.1 us)
Async XLA Ops:
  7.2 89.6 %all-gather.10.cloned.1.call-start = ((), (), s32[]{:S(2)}) async-start(), calls=%async_computation.4 | async-start | bytes 4718592 | tf_op jit(solution)/shard_map/all_gather | solution.py:42
  7.2 3.5 copy-start.15
  10.6 2.1 copy-start
  11.7 9.4 %copy-start.7 = (f32[128,8,8,128]{3,2,1,0:T(8,128)}, f32[128,8,8,128]{3,2,1,0:T(8,128)S(1)}, u32[]{:S(2)}) copy-start(f32[128,8,8,128]{3,2,1,0:T(8,128)S(1)} %copy.94) | copy-start | bytes 12582916
  21.1 197.1 %all-gather.6.cloned.1.call-start = ((), (), s32[]{:S(2)}) async-start(), calls=%async_computation.1 | async-start | bytes 20971520 | tf_op jit(solution)/shard_map/all_gather | solution.py:65
  21.3 5.3 copy-start.8
  24.7 2.0 copy-start.3
  26.7 16.0 %copy-start.1 = (f32[128,8,8,128]{3,2,1,0:T(8,128)S(1)}, f32[128,8,8,128]{3,2,1,0:T(8,128)}, u32[]{:S(2)}) copy-start(f32[128,8,8,128]{3,2,1,0:T(8,128)} %copy-done) | copy-start | bytes 12582916
  73.7 29.7 %copy-start.14 = (f32[8,128,128]{2,1,0:T(8,128)S(1)}, f32[8,128,128]{2,1,0:T(8,128)}, u32[]{:S(2)}) copy-start(f32[8,128,128]{2,1,0:T(8,128)} %get-tuple-element.11) | copy-start | bytes 1572868
  96.8 6.9 %copy-start.4 = (f32[128,8,8,128]{3,2,1,0:T(8,128)S(1)}, f32[128,8,8,128]{3,2,1,0:T(8,128)}, u32[]{:S(2)}) copy-start(f32[128,8,8,128]{3,2,1,0:T(8,128)} %copy-done.3) | copy-start | bytes 12582916
  96.8 6.9 %copy-start.11 = (f32[2,8,512,128]{3,2,1,0:T(8,128)S(1)}, f32[2,8,512,128]{3,2,1,0:T(8,128)}, u32[]{:S(2)}) copy-start(f32[2,8,512,128]{3,2,1,0:T(8,128)} %fusion) | copy-start | bytes 12582916
  103.7 4.4 copy-start.13
  113.6 243.7 %all-gather.8.cloned.1.call-start = ((), (), s32[]{:S(2)}) async-start(), calls=%async_computation.3 | async-start | bytes 4718592 | tf_op jit(solution)/shard_map/all_gather | solution.py:41
  114.1 3.5 copy-start.5
  117.4 9.5 %copy-start.6 = (f32[128,8,8,128]{3,2,1,0:T(8,128)}, f32[128,8,8,128]{3,2,1,0:T(8,128)S(1)}, u32[]{:S(2)}) copy-start(f32[128,8,8,128]{3,2,1,0:T(8,128)S(1)} %copy.91) | copy-start | bytes 12582916
  127.0 448.1 %reduce-scatter.2.cloned.1.call-start = ((), (), s32[]{:S(2)}) async-start(), calls=%async_computation.2 | async-start | bytes 18874368 | tf_op jit(solution)/shard_map/reduce_scatter | solution.py:66
  352.8 11.1 %copy-start.12 = (f32[2,8,128,128]{3,2,1,0:T(8,128)S(1)}, f32[2,8,128,128]{3,2,1,0:T(8,128)}, u32[]{:S(2)}) copy-start(f32[2,8,128,128]{3,2,1,0:T(8,128)} %get-tuple-element.10) | copy-start | bytes 3145732
  357.3 7.2 %copy-start.2 = (f32[128,8,8,128]{3,2,1,0:T(8,128)S(1)}, f32[128,8,8,128]{3,2,1,0:T(8,128)}, u32[]{:S(2)}) copy-start(f32[128,8,8,128]{3,2,1,0:T(8,128)} %copy-done) | copy-start | bytes 12582916
  357.3 7.2 %copy-start.9 = (f32[2,8,512,128]{3,2,1,0:T(8,128)S(1)}, f32[2,8,512,128]{3,2,1,0:T(8,128)}, u32[]{:S(2)}) copy-start(f32[2,8,512,128]{3,2,1,0:T(8,128)} %fusion.4) | copy-start | bytes 12582916
  368.9 2.5 copy-start.10
  371.4 205.8 %copy-start.19 = (f32[1,512]{1,0:T(1,128)S(1)}, f32[1,512]{1,0:T(1,128)}, u32[]{:S(2)}) copy-start(f32[1,512]{1,0:T(1,128)} %param.12) | copy-start | bytes 6148
  371.4 207.1 %copy-start.18 = (f32[1,1024]{1,0:T(1,128)S(1)}, f32[1,1024]{1,0:T(1,128)}, u32[]{:S(2)}) copy-start(f32[1,1024]{1,0:T(1,128)} %param.13) | copy-start | bytes 12292
  577.8 4.0 copy-start.17
  578.5 3.3 copy-start.16
Sparse Core Ops, SparseCore 0:
  21.2 75.5 all-gather.9
  113.7 104.4 all-gather.5
  220.3 72.7 all-gather.7
  296.8 278.2 reduce-scatter.1
where the time goes:
time: 596 us; the launch traced here: 589 us
  waiting for transfers between devices  313 us (53%)
  matrix products  222 us (37%)
  local copies, waits for them, and re-layouts  31.8 us (5%)
  between operations  15.2 us (3%)
  other arithmetic  6.94 us (1%)
    reduce_scatter x1, waiting for transfers between devices, shards(): lax.psum_scatter(lax.dot_general(value_whole, inputs, (((0,), (0,)), ((),...  198 us
    all_gather x1, waiting for transfers between devices, shards(): value_whole = lax.all_gather(value_grad, 'head', axis=1, tiled=True)  91.1 us
    dot_general x1, matrix products, shards(): lax.dot_general(value_whole, inputs, (((0,), (0,)), ((), ())), precision=...  59.7 us
    dot_general x1, matrix products, shards(): jnp.einsum('nhts,nthd->nshd', query_key, grad_blocks, precision=highest)  31.1 us
    dot_general x1, matrix products, shards(): jnp.einsum('nhts,nthd->nshd', grad_value, query_blocks, precision=highest)  30.1 us
    all_gather x1, waiting for transfers between devices, shards(): lax.all_gather(local_rev[None], 'seq', axis=0, tiled=True)  23.1 us
    dot_general x1, matrix products, shards(): jnp.einsum('nthd,nshd->nhts', grad_blocks, value_blocks, precision=highest)  18.8 us
    dot_general x1, matrix products, shards(): jnp.einsum('nhts,nshd->nthd', grad_value, key_blocks, precision=highest)  18.3 us
  transfers between devices with their start and end apart: 4, of which 3 were waited for; matrix products, arithmetic and copies ran while one was open for 38% of the time, Pallas kernels for 0%

commit v1 on v0

--- a/solution.py
+++ b/solution.py
@@ -62,7 +62,15 @@
     query_grad = (attn_scale * query_grad).reshape(tok_count, feat_width)
     key_grad = (attn_scale * key_grad).reshape(tok_count, feat_width)
     value_grad = (attn_scale * value_grad).reshape(tok_count, feat_width)
-    value_whole = lax.all_gather(value_grad, "head", axis=1, tiled=True)
+    ways, here = (lax.axis_size("head"), lax.axis_index("head"))
+    grown, reach = (value_grad, 1)
+    while reach < ways:
+        theirs = lax.ppermute(grown, "head", [(d, d ^ reach) for d in range(ways)])
+        mine_first = jnp.concatenate([grown, theirs], axis=1)
+        theirs_first = jnp.concatenate([theirs, grown], axis=1)
+        grown = jnp.where(here & reach == 0, mine_first, theirs_first)
+        reach = 2 * reach
+    value_whole = grown
     weight_grad = lax.psum_scatter(
         lax.dot_general(
             value_whole,

time: 596 us -> 677 us (1.14)
  waiting for transfers between devices: 313 us -> 378 us
  other arithmetic: 6.94 us -> 17.4 us
    ppermute x0 -> x2, waiting for transfers between devices: none -> 177 us  [shards(): theirs = lax.ppermute(grown, 'head', [(d, d ^ reach) for d in range(ways)])]
    all_gather x1 -> x0, waiting for transfers between devices: 91.1 us -> none  [shards(): value_whole = lax.all_gather(value_grad, 'head', axis=1, tiled=True)]
    reduce_scatter x1, waiting for transfers between devices: 198 us -> 179 us  [shards(): lax.psum_scatter(lax.dot_general(value_whole, inputs, (((0,), (0,)), ((),...]
    select_n x0 -> x1, other arithmetic: none -> 10.5 us  [shards(): grown = jnp.where(here & reach == 0, mine_first, theirs_first)]
    unnamed x45 -> x47, local copies, waits for them, and re-layouts: 17.1 us -> 16.4 us
  transfers between devices with their start and end apart: 4 -> 5, of which waited for: 3 -> 4; matrix products, arithmetic and copies ran while one was open for 38% -> 33% of each run, Pallas kernels for 0% -> 0%
where the time goes in v1:
time: 677 us; the launch traced here: 670 us
  waiting for transfers between devices  378 us (56%)
  matrix products  226 us (33%)
  local copies, waits for them, and re-layouts  31.2 us (5%)
  other arithmetic  17.4 us (3%)
  between operations  15 us (2%)
    reduce_scatter x1, waiting for transfers between devices, shards(): lax.psum_scatter(lax.dot_general(value_whole, inputs, (((0,), (0,)), ((),...  179 us
    ppermute x2, waiting for transfers between devices, shards(): theirs = lax.ppermute(grown, 'head', [(d, d ^ reach) for d in range(ways)])  177 us
    dot_general x1, matrix products, shards(): lax.dot_general(value_whole, inputs, (((0,), (0,)), ((), ())), precision=...  63.2 us
    dot_general x1, matrix products, shards(): jnp.einsum('nhts,nthd->nshd', query_key, grad_blocks, precision=highest)  31 us
    dot_general x1, matrix products, shards(): jnp.einsum('nhts,nthd->nshd', grad_value, query_blocks, precision=highest)  30.5 us
    all_gather x1, waiting for transfers between devices, shards(): lax.all_gather(local_rev[None], 'seq', axis=0, tiled=True)  22.8 us
    dot_general x1, matrix products, shards(): jnp.einsum('nthd,nshd->nhts', grad_blocks, value_blocks, precision=highest)  18.9 us
    dot_general x1, matrix products, shards(): jnp.einsum('nhts,nshd->nthd', grad_value, key_blocks, precision=highest)  18.3 us
  transfers between devices with their start and end apart: 5, of which 4 were waited for; matrix products, arithmetic and copies ran while one was open for 33% of the time, Pallas kernels for 0%

profile of v1, /device:TPU:0, one launch (start us, length us, event | category | flops | bytes accessed | tf_op | source)
XLA Modules:
  0.0 669.7 jit_solution(12100726112617702734)
XLA Ops:
  7.2 0.0 all-gather.7.cloned.1.call-start
  7.2 3.4 copy.90
  10.6 0.1 copy-done.15
  10.7 1.0 copy.94
  11.7 0.9 copy-done
  12.7 8.4 %fusion.65 = (f32[8,128,128]{2,1,0:T(8,128)}, f32[2,8,128,128]{3,2,1,0:T(8,128)S(1)}) fusion(f32[2,512,8,128]{3,2,1,0:T(8,128)S(1)} %bitcast.70, f32[2,512,8,128]{3,2,1,0:T(8,128)S(1)} %bitcast.81), kind=kOutput, calls=%fused_computation.76 | convolution fusion | flops 1610743808 | bytes 9961472 | tf_op jit(solution)/shard_map/ntha,nthb->nhab/dot_general | solution.py:37
  21.1 0.0 all-gather.7.cloned.1.call-update
  21.1 0.5 all-gather.5.cloned.1.call-start
  21.7 3.4 copy.92
  25.0 0.1 fusion.53
  25.2 1.8 copy-done.3
  27.0 16.0 %fusion.25 = f32[2,8,512,512]{3,2,1,0:T(8,128)} fusion(f32[2,512,8,128]{3,2,1,0:T(8,128)S(1)} %bitcast.83, f32[2,512,8,128]{3,2,1,0:T(8,128)S(1)} %bitcast.74), kind=kOutput, calls=%fused_computation.33 | convolution fusion | flops 6442450944 | bytes 25165824 | tf_op jit(solution)/shard_map/nthd,nshd->nhts/dot_general | solution.py:34
  42.9 31.0 %fusion.6 = f32[2,8,512,128]{3,2,1,0:T(8,128)} fusion(f32[2,8,512,512]{3,2,1,0:T(8,128)} %fusion.25, f32[512,512]{1,0:T(8,128)S(1)} %fusion.53, f32[2,512,8,128]{3,2,1,0:T(8,128)S(1)} %bitcast.72), kind=kOutput, calls=%fused_computation.7 | convolution fusion | flops 6446645248 | bytes 26214400 | tf_op jit(solution)/shard_map/nhts,nthd->nshd/dot_general | solution.py:58
  74.0 22.8 %all-gather.7.cloned.1.call-done = f32[64,128,128]{2,1,0:T(8,128)} async-done(((f32[8,128,128]{2,1,0:T(8,128)}), f32[64,128,128]{2,1,0:T(8,128)}) %all-gather.7.cloned.1.call-update) | async-done | bytes 4194320 | tf_op jit(solution)/shard_map/all_gather | solution.py:42
  96.8 6.6 fusion.19
  103.4 0.1 add.38
  103.5 0.2 reduce-window_subtract_fusion
  103.7 0.0 copy-start.13
  103.8 4.4 fusion.16
  108.2 2.4 copy.76
  110.6 3.0 copy.146
  113.6 7.5 %collective-permute-done = f32[1024,1024]{1,0:T(8,128)} collective-permute-done((f32[1024,1024]{1,0:T(8,128)}, f32[1024,1024]{1,0:T(8,128)}, u32[]{:S(2)}, u32[]{:S(2)}) %collective-permute-start) | collective-permute-done | bytes 4194336 | tf_op jit(solution)/shard_map/ppermute | solution.py:68
  121.1 10.5 %maximum_select_fusion.2 = f32[1024,2048]{1,0:T(8,128)} fusion(f32[1024,1024]{1,0:T(8,128)} %collective-permute-done, f32[1024,1024]{1,0:T(8,128)} %bitcast.69, pred[]{:T(512)S(6)} %eq.7), kind=kLoop, calls=%fused_computation.13 | loop fusion | flops 6291456 | bytes 16777216 | tf_op jit(solution)/shard_map/jit(_where)/select_n | solution.py:71
  131.6 1.5 collective-permute-start.1
  133.2 1.0 copy.91
  134.2 0.0 copy-start.6
  134.2 1.6 copy-done.5
  135.9 9.5 %fusion.64 = (f32[8,128,128]{2,1,0:T(8,128)}, f32[2,8,128,128]{3,2,1,0:T(8,128)}) fusion(f32[2,512,8,128]{3,2,1,0:T(8,128)S(1)} %bitcast.77, f32[2,512,8,128]{3,2,1,0:T(8,128)S(1)} %bitcast.78), kind=kOutput, calls=%fused_computation.75 | convolution fusion | flops 1610743808 | bytes 9961472 | tf_op jit(solution)/shard_map/nsha,nshb->nhab/dot_general | solution.py:36
  145.3 0.0 all-gather.5.cloned.1.call-update
  145.3 0.0 reduce-scatter.2.cloned.1.call-start
  145.4 169.1 %collective-permute-done.1 = f32[1024,2048]{1,0:T(8,128)} collective-permute-done((f32[1024,2048]{1,0:T(8,128)}, f32[1024,2048]{1,0:T(8,128)}, u32[]{:S(2)}, u32[]{:S(2)}) %collective-permute-start.1) | collective-permute-done | bytes 8388640 | tf_op jit(solution)/shard_map/ppermute | solution.py:68
  314.5 63.2 %fusion = f32[4096,1024]{1,0:T(8,128)} fusion(f32[1024,1024]{1,0:T(8,128)} %param.11, f32[1024,2048]{1,0:T(8,128)} %collective-permute-done.1, f32[1024,2048]{1,0:T(8,128)} %maximum_select_fusion.2, pred[]{:T(512)S(6)} %eq.6), kind=kOutput, calls=%fused_computation.1 | convolution fusion | flops 51552190464 | bytes 37748736 | tf_op jit(solution)/shard_map/dot_general | solution.py:75
  377.7 0.0 reduce-scatter.2.cloned.1.call-update
  377.7 18.9 %fusion.32 = f32[2,8,512,512]{3,2,1,0:T(8,128)S(1)} fusion(f32[2,512,8,128]{3,2,1,0:T(8,128)} %bitcast.79, f32[2,512,8,128]{3,2,1,0:T(8,128)} %bitcast.71), kind=kOutput, calls=%fused_computation.40 | convolution fusion | flops 6442450944 | bytes 25165824 | tf_op jit(solution)/shard_map/nthd,nshd->nhts/dot_general | solution.py:31
  396.6 30.5 %fusion.8 = f32[2,8,512,128]{3,2,1,0:T(8,128)} fusion(f32[2,8,512,512]{3,2,1,0:T(8,128)S(1)} %fusion.32, f32[512,512]{1,0:T(8,128)S(1)} %fusion.53, f32[2,512,8,128]{3,2,1,0:T(8,128)} %bitcast.82), kind=kOutput, calls=%fused_computation.9 | convolution fusion | flops 6446645248 | bytes 26214400 | tf_op jit(solution)/shard_map/nhts,nthd->nshd/dot_general | solution.py:56
  427.2 18.3 %fusion.10 = f32[2,8,512,128]{3,2,1,0:T(8,128)} fusion(f32[2,8,512,512]{3,2,1,0:T(8,128)S(1)} %fusion.32, f32[512,512]{1,0:T(8,128)S(1)} %fusion.53, f32[2,512,8,128]{3,2,1,0:T(8,128)} %bitcast.75), kind=kOutput, calls=%fused_computation.11 | convolution fusion | flops 6446645248 | bytes 26214400 | tf_op jit(solution)/shard_map/nhts,nshd->nthd/dot_general | solution.py:52
  445.5 7.8 %fusion.17 = f32[2,512,8,128]{3,1,2,0:T(8,128)S(1)} fusion(f32[2,8,512,128]{3,2,1,0:T(8,128)} %fusion.8, f32[2,8,128,128]{3,2,1,0:T(8,128)} %copy-done.13, f32[2,512,8,128]{3,2,1,0:T(8,128)} %bitcast.80), kind=kOutput, calls=%fused_computation.24 | convolution fusion | flops 1612709888 | bytes 13631488 | tf_op jit(solution)/shard_map/nshb,nhab->nsha/dot_general | solution.py:57
  453.3 4.4 copy.68
  457.7 6.7 fusion.21
  464.4 0.5 fusion.52
  464.9 4.4 fusion.18
  469.4 2.4 copy.61
  471.8 5.5 copy_bitcast_fusion.1
  477.3 178.9 %reduce-scatter.2.cloned.1.call-done = f32[512,1024]{1,0:T(8,128)} async-done(((f32[4096,1024]{1,0:T(8,128)}), f32[512,1024]{1,0:T(8,128)}) %reduce-scatter.2.cloned.1.call-update) | async-done | bytes 2097168 | tf_op jit(solution)/shard_map/reduce_scatter | solution.py:74
  656.2 2.1 fusion.50
  658.3 0.6 fusion.63
  659.6 0.0 copy-start.17
  659.6 3.3 rsqrt_multiply_fusion
  (40 shorter events, 0.1 us)
Async XLA Ops:
  7.2 89.6 %all-gather.7.cloned.1.call-start = ((), (), s32[]{:S(2)}) async-start(), calls=%async_computation.3 | async-start | bytes 4718592 | tf_op jit(solution)/shard_map/all_gather | solution.py:42
  7.2 3.5 copy-start.15
  10.6 2.1 copy-start
  11.7 9.4 %copy-start.7 = (f32[128,8,8,128]{3,2,1,0:T(8,128)}, f32[128,8,8,128]{3,2,1,0:T(8,128)S(1)}, u32[]{:S(2)}) copy-start(f32[128,8,8,128]{3,2,1,0:T(8,128)S(1)} %copy.94) | copy-start | bytes 12582916
  21.1 436.6 %all-gather.5.cloned.1.call-start = ((), (), s32[]{:S(2)}) async-start(), calls=%async_computation.2 | async-start | bytes 4718592 | tf_op jit(solution)/shard_map/all_gather | solution.py:41
  21.6 5.3 copy-start.8
  25.0 2.0 copy-start.3
  27.0 16.0 %copy-start.1 = (f32[128,8,8,128]{3,2,1,0:T(8,128)S(1)}, f32[128,8,8,128]{3,2,1,0:T(8,128)}, u32[]{:S(2)}) copy-start(f32[128,8,8,128]{3,2,1,0:T(8,128)} %copy-done) | copy-start | bytes 12582916
  74.0 29.4 %copy-start.14 = (f32[8,128,128]{2,1,0:T(8,128)S(1)}, f32[8,128,128]{2,1,0:T(8,128)}, u32[]{:S(2)}) copy-start(f32[8,128,128]{2,1,0:T(8,128)} %get-tuple-element.11) | copy-start | bytes 1572868
  96.8 6.9 %copy-start.4 = (f32[128,8,8,128]{3,2,1,0:T(8,128)S(1)}, f32[128,8,8,128]{3,2,1,0:T(8,128)}, u32[]{:S(2)}) copy-start(f32[128,8,8,128]{3,2,1,0:T(8,128)} %copy-done.3) | copy-start | bytes 12582916
  96.8 6.9 %copy-start.11 = (f32[2,8,512,128]{3,2,1,0:T(8,128)S(1)}, f32[2,8,512,128]{3,2,1,0:T(8,128)}, u32[]{:S(2)}) copy-start(f32[2,8,512,128]{3,2,1,0:T(8,128)} %fusion.6) | copy-start | bytes 12582916
  103.7 4.4 copy-start.13
  113.6 7.5 %collective-permute-start = (f32[1024,1024]{1,0:T(8,128)}, f32[1024,1024]{1,0:T(8,128)}, u32[]{:S(2)}, u32[]{:S(2)}) collective-permute-start(f32[1024,1024]{1,0:T(8,128)} %bitcast.69), channel_id=1, source_target_pairs={{0,1},{1,0},{2,3},{3,2},{4,5},{5,4},{6,7},{7,6},{8,9},{9,8},{10,11... | collective-permute-start | bytes 12582920 | tf_op jit(solution)/shard_map/ppermute | solution.py:68
  113.6 19.5 %copy-start.16 = (f32[1024,1024]{1,0:T(8,128)S(1)}, f32[1024,1024]{1,0:T(8,128)}, u32[]{:S(2)}) copy-start(f32[1024,1024]{1,0:T(8,128)} %param.9) | copy-start | bytes 12582916
  131.6 182.9 %collective-permute-start.1 = (f32[1024,2048]{1,0:T(8,128)}, f32[1024,2048]{1,0:T(8,128)}, u32[]{:S(2)}, u32[]{:S(2)}) collective-permute-start(f32[1024,2048]{1,0:T(8,128)} %maximum_select_fusion.2), channel_id=1, source_target_pairs={{0,2},{1,3},{2,0},{3,1},{4,6},{5,7},{6,4},{7,5},{8,10},{9,11},{10,... | collective-permute-start | bytes 25165832 | tf_op jit(solution)/shard_map/ppermute | solution.py:68
  133.2 2.7 copy-start.5
  134.2 11.1 %copy-start.6 = (f32[128,8,8,128]{3,2,1,0:T(8,128)}, f32[128,8,8,128]{3,2,1,0:T(8,128)S(1)}, u32[]{:S(2)}) copy-start(f32[128,8,8,128]{3,2,1,0:T(8,128)S(1)} %copy.91) | copy-start | bytes 12582916
  145.3 510.9 %reduce-scatter.2.cloned.1.call-start = ((), (), s32[]{:S(2)}) async-start(), calls=%async_computation.1 | async-start | bytes 18874368 | tf_op jit(solution)/shard_map/reduce_scatter | solution.py:74
  453.3 11.1 %copy-start.12 = (f32[2,8,128,128]{3,2,1,0:T(8,128)S(1)}, f32[2,8,128,128]{3,2,1,0:T(8,128)}, u32[]{:S(2)}) copy-start(f32[2,8,128,128]{3,2,1,0:T(8,128)} %get-tuple-element.10) | copy-start | bytes 3145732
  457.7 7.2 %copy-start.2 = (f32[128,8,8,128]{3,2,1,0:T(8,128)S(1)}, f32[128,8,8,128]{3,2,1,0:T(8,128)}, u32[]{:S(2)}) copy-start(f32[128,8,8,128]{3,2,1,0:T(8,128)} %copy-done) | copy-start | bytes 12582916
  457.7 7.2 %copy-start.9 = (f32[2,8,512,128]{3,2,1,0:T(8,128)S(1)}, f32[2,8,512,128]{3,2,1,0:T(8,128)}, u32[]{:S(2)}) copy-start(f32[2,8,512,128]{3,2,1,0:T(8,128)} %fusion.10) | copy-start | bytes 12582916
  469.4 2.5 copy-start.10
  471.8 186.5 %copy-start.20 = (f32[1,512]{1,0:T(1,128)S(1)}, f32[1,512]{1,0:T(1,128)}, u32[]{:S(2)}) copy-start(f32[1,512]{1,0:T(1,128)} %param.12) | copy-start | bytes 6148
  471.8 187.7 %copy-start.19 = (f32[1,1024]{1,0:T(1,128)S(1)}, f32[1,1024]{1,0:T(1,128)}, u32[]{:S(2)}) copy-start(f32[1,1024]{1,0:T(1,128)} %param.13) | copy-start | bytes 12292
  658.9 4.0 copy-start.18
  659.6 3.3 copy-start.17
Sparse Core Ops, SparseCore 0:
  21.2 75.4 all-gather.6
  145.5 70.4 all-gather.4
  377.9 278.2 reduce-scatter.1
